TPU v7x, 32 devices: a whole 2x2x4 slice. The times are simulated.
32 devices in a mesh: patch: 2 (over x), epoch: 16 (over z, y, core).
Axes of the slice: x: 2, y: 2, z: 4, core: 2. Of those that a mesh axis runs over, the one named last changes fastest.
Arguments:
- images: float32 [32, 128, 1024], P(('patch', 'epoch')), parts along dimension 0, may hold values from -20 to 20, as said below
- variance: float32 [32], P(('patch', 'epoch')), parts along dimension 0, may hold values from 0.25 to 4
- zero_point: float32 [32], P(('patch', 'epoch')), parts along dimension 0, may hold values from 0.5 to 2
- block_mask: int32 [32, 1], P(('patch', 'epoch')), parts along dimension 0, may hold values 0 or 1
- stamps: int32 [32, 512], P(('patch', 'epoch')), parts along dimension 0, may hold values from 0 to 131071
- owners: int32 [8], P('patch'), parts along dimension 0, may hold values from 0 to 15
Outputs:
- significance: float32 [32, 128, 1024], P(('patch', 'epoch')), parts along dimension 0
- coefficients: float32 [32, 15], P(('patch', 'epoch')), parts along dimension 0
There are 2 independent parts, one for each index of `patch`. A program takes and returns all parts, laid end to end along the dimension named above; each array names one. Nothing has to cross between parts.
Inputs may be any that keep to these rules, and one draw needn't show every extreme that they name: `images`: each epoch is a common sky times an epoch scale plus noise.
All inputs are finite; a program needn't handle non-finite values. No bound on the sum of `block_mask` on one device may be relied on, other than what follows from the above.
Results may differ from a plain program's by a relative error of at most 0.00075.
The roundings to bfloat16 on the way count: a program that leaves them out, or rounds other values in their place, can miss the bound.
Values sent between devices are 32-bit elements; how exact they have to be, the bound alone decides.
A program may use at most 64 MiB of HBM per device.

v0:
```python
import math
import jax
import jax.numpy as jnp
from jax import lax
from jax.sharding import PartitionSpec as P

TILES = 4
KHALF = 7
NBASIS = 12
sigma_list = (0.75, 1.5, 3.0)
basis_pairs = ((0, 0), (2, 0), (0, 2), (1, 1))


def raise_power(scaled, degree):
    result = jnp.ones_like(scaled)
    for step in range(degree):
        result = result * scaled
    return result


def tap_values(offset, sigma, degree):
    scaled = offset / sigma
    value = (
        jnp.exp(-0.5 * scaled * scaled)
        * raise_power(scaled, degree)
        / (math.sqrt(2.0 * math.pi) * sigma)
    )
    value = jnp.where(jnp.abs(offset) <= KHALF, value, 0.0)
    return value.astype(jnp.bfloat16)


def band_matrix(count, sigma, degree, along_cols):
    index = jnp.arange(count, dtype=jnp.int32)
    if along_cols:
        offset = index[:, None] - index[None, :]
    else:
        offset = index[None, :] - index[:, None]
    return tap_values(offset.astype(jnp.float32), sigma, degree)


def shards(images, variance, zero_point, block_mask, stamps, owners):
    image = images[0]
    rows_all, cols_all = image.shape
    count = lax.axis_size("epoch")
    weight = 1.0 / variance[0]
    mask_f = block_mask[0].astype(jnp.float32)
    block_term = weight * mask_f
    numer = jnp.repeat(block_term, 128)[:, None] * image
    scales_all = lax.all_gather(zero_point, "epoch", axis=0, tiled=True)
    owner_scale = jnp.sum(
        (owners[:, None] == jnp.arange(count)[None, :]).astype(jnp.float32) * scales_all[None, :],
        axis=1,
    )
    col_scale = jnp.repeat(owner_scale, cols_all // TILES)
    stamp_row = stamps[0]
    numer_sum, block_sum = lax.psum((numer, block_term), "epoch")
    den_rows = jnp.repeat(1.0 + block_sum, 128)
    reference_img = numer_sum / den_rows[:, None] * col_scale[None, :]
    stamp_ref = jnp.take(reference_img.reshape(-1), stamp_row)
    sharp = image.astype(jnp.bfloat16)
    bases = []
    for sigma in sigma_list:
        across = {}
        for degree in (0, 1, 2):
            across[degree] = jnp.dot(
                sharp,
                band_matrix(cols_all, sigma, degree, True),
                preferred_element_type=jnp.float32,
            ).astype(jnp.bfloat16)
        for pair in basis_pairs:
            vertical = band_matrix(rows_all, sigma, pair[1], False)
            bases.append(
                jnp.dot(vertical, across[pair[0]], preferred_element_type=jnp.float32).astype(
                    jnp.bfloat16
                )
            )
    xn = 2.0 * (jnp.arange(cols_all).astype(jnp.float32) + 0.5) / cols_all - 1.0
    yn = 2.0 * (jnp.arange(rows_all).astype(jnp.float32) + 0.5) / rows_all - 1.0
    picks = [jnp.take(b.reshape(-1), stamp_row).astype(jnp.float32) for b in bases]
    picks = picks + [
        jnp.ones(stamp_row.shape, jnp.float32),
        xn[stamp_row % cols_all],
        yn[stamp_row // cols_all],
    ]
    design = jnp.stack(picks, axis=0)
    normal = jnp.dot(design, design.T, precision=lax.Precision.HIGHEST)
    normal = normal + 0.05 * jnp.diag(jnp.diag(normal))
    rhs = jnp.dot(design, stamp_ref, precision=lax.Precision.HIGHEST)
    factor = jnp.linalg.cholesky(normal)
    coef = jax.scipy.linalg.cho_solve((factor, True), rhs)
    model = jnp.zeros((rows_all, cols_all), jnp.float32)
    for index in range(NBASIS):
        model = model + coef[index] * bases[index].astype(jnp.float32)
    model = model + coef[NBASIS] + coef[NBASIS + 1] * xn[None, :] + coef[NBASIS + 2] * yn[:, None]
    diff = jnp.repeat(mask_f, 128)[:, None] * (model - reference_img)
    pooled = lax.psum(diff * diff, "epoch")
    scatter = jnp.sqrt(0.05 + pooled / count)
    result = diff / scatter
    return (result[None], coef[None])


def solution(mesh):
    in_specs = (
        P(("patch", "epoch"), None, None),
        P(("patch", "epoch")),
        P(("patch", "epoch")),
        P(("patch", "epoch"), None),
        P(("patch", "epoch"), None),
        P("patch"),
    )
    out_specs = (P(("patch", "epoch"), None, None), P(("patch", "epoch"), None))
    return jax.shard_map(shards, mesh=mesh, in_specs=in_specs, out_specs=out_specs, check_vma=False)
```

profile of v0, /device:TPU:0, one launch (start us, length us, event | category | flops | bytes accessed | tf_op | source)
XLA Modules:
  0.0 242.0 jit_solution(10815017619409974044)
XLA Ops:
  8.5 2.2 fusion.182
  10.8 2.3 fusion.11
  13.1 2.2 fusion.15
  15.3 2.4 fusion.14
  18.2 2.3 fusion.18
  20.5 2.2 fusion.22
  22.6 2.6 %fusion.21 = bf16[128,1024]{1,0:T(8,128)(2,1)S(1)} fusion(bf16[1,128,1024]{2,1,0:T(8,128)(2,1)S(1)} %get-tuple-element.11), kind=kOutput, calls=%fused_computation.54 | convolution fusion | flops 314998784 | bytes 524288 | tf_op jit(solution)/shard_map/dot_general | solution.py:73
  25.7 3.0 %fusion.25 = bf16[128,1024]{1,0:T(8,128)(2,1)} fusion(bf16[1,128,1024]{2,1,0:T(8,128)(2,1)S(1)} %get-tuple-element.11), kind=kOutput, calls=%fused_computation.58 | convolution fusion | flops 313966592 | bytes 524288 | tf_op jit(solution)/shard_map/dot_general | solution.py:73
  28.7 2.2 fusion.29
  30.9 3.1 %fusion.28 = bf16[128,1024]{1,0:T(8,128)(2,1)} fusion(bf16[1,128,1024]{2,1,0:T(8,128)(2,1)S(1)} %get-tuple-element.11), kind=kOutput, calls=%fused_computation.61 | convolution fusion | flops 314998784 | bytes 524288 | tf_op jit(solution)/shard_map/dot_general | solution.py:73
  36.5 36.3 %all-reduce.1 = (f32[16]{0:T(128)S(1)}, f32[1]{0:T(128)}) all-reduce(f32[16]{0:T(128)S(1)} %dynamic-update-slice.3, f32[1]{0:T(128)} %mul.385), channel_id=1, replica_groups=mesh['patch'=2,'epoch'=16] {'epoch'}, use_global_device_ids=true, to_apply=%add | all-reduce | flops 17 | bytes 136
  73.9 3.5 %gather_fusion.15 = bf16[512]{0:T(512)(128)(2,1)S(1)} fusion(bf16[131072]{0:T(1024)(128)(2,1)S(1)} %bitcast.149, s32[1024]{0:T(1024)S(1)} %pad_clamp_fusion.3), kind=kCustom, calls=%fused_computation.11.clone | custom fusion | bytes 4096 | tf_op jit(solution)/shard_map/jit(_take)/gather | solution.py:79
  77.4 3.5 %gather_fusion.14 = bf16[512]{0:T(512)(128)(2,1)S(1)} fusion(bf16[131072]{0:T(1024)(128)(2,1)S(1)} %bitcast.148, s32[1024]{0:T(1024)S(1)} %pad_clamp_fusion.3), kind=kCustom, calls=%fused_computation.10.clone | custom fusion | bytes 4096 | tf_op jit(solution)/shard_map/jit(_take)/gather | solution.py:79
  81.0 3.5 %gather_fusion.13 = bf16[512]{0:T(512)(128)(2,1)S(1)} fusion(bf16[131072]{0:T(1024)(128)(2,1)S(1)} %bitcast.151, s32[1024]{0:T(1024)S(1)} %pad_clamp_fusion.3), kind=kCustom, calls=%fused_computation.9.clone | custom fusion | bytes 4096 | tf_op jit(solution)/shard_map/jit(_take)/gather | solution.py:79
  84.6 3.5 %gather_fusion.12 = bf16[512]{0:T(512)(128)(2,1)S(1)} fusion(bf16[131072]{0:T(1024)(128)(2,1)S(1)} %bitcast.152, s32[1024]{0:T(1024)S(1)} %pad_clamp_fusion.3), kind=kCustom, calls=%fused_computation.8.clone | custom fusion | bytes 4096 | tf_op jit(solution)/shard_map/jit(_take)/gather | solution.py:79
  88.1 3.5 %gather_fusion.11 = bf16[512]{0:T(512)(128)(2,1)S(1)} fusion(bf16[131072]{0:T(1024)(128)(2,1)S(1)} %bitcast.153, s32[1024]{0:T(1024)S(1)} %pad_clamp_fusion.3), kind=kCustom, calls=%fused_computation.7.clone | custom fusion | bytes 4096 | tf_op jit(solution)/shard_map/jit(_take)/gather | solution.py:79
  91.7 3.5 %gather_fusion.10 = bf16[512]{0:T(512)(128)(2,1)S(1)} fusion(bf16[131072]{0:T(1024)(128)(2,1)S(1)} %bitcast.154, s32[1024]{0:T(1024)S(1)} %pad_clamp_fusion.3), kind=kCustom, calls=%fused_computation.6.clone | custom fusion | bytes 4096 | tf_op jit(solution)/shard_map/jit(_take)/gather | solution.py:79
  95.3 3.5 %gather_fusion.9 = bf16[512]{0:T(512)(128)(2,1)S(1)} fusion(bf16[131072]{0:T(1024)(128)(2,1)S(1)} %bitcast.155, s32[1024]{0:T(1024)S(1)} %pad_clamp_fusion.3), kind=kCustom, calls=%fused_computation.5.clone | custom fusion | bytes 4096 | tf_op jit(solution)/shard_map/jit(_take)/gather | solution.py:79
  98.9 3.5 %gather_fusion.8 = bf16[512]{0:T(512)(128)(2,1)S(1)} fusion(bf16[131072]{0:T(1024)(128)(2,1)S(1)} %bitcast.156, s32[1024]{0:T(1024)S(1)} %pad_clamp_fusion.3), kind=kCustom, calls=%fused_computation.4.clone | custom fusion | bytes 4096 | tf_op jit(solution)/shard_map/jit(_take)/gather | solution.py:79
  102.5 3.5 %gather_fusion.7 = bf16[512]{0:T(512)(128)(2,1)S(1)} fusion(bf16[131072]{0:T(1024)(128)(2,1)S(1)} %bitcast.157, s32[1024]{0:T(1024)S(1)} %pad_clamp_fusion.3), kind=kCustom, calls=%fused_computation.3.clone | custom fusion | bytes 4096 | tf_op jit(solution)/shard_map/jit(_take)/gather | solution.py:79
  106.0 3.5 %gather_fusion.6 = bf16[512]{0:T(512)(128)(2,1)S(1)} fusion(bf16[131072]{0:T(1024)(128)(2,1)S(1)} %bitcast.158, s32[1024]{0:T(1024)S(1)} %pad_clamp_fusion.3), kind=kCustom, calls=%fused_computation.2.clone | custom fusion | bytes 4096 | tf_op jit(solution)/shard_map/jit(_take)/gather | solution.py:79
  109.6 3.5 %gather_fusion.5 = bf16[512]{0:T(512)(128)(2,1)S(1)} fusion(bf16[131072]{0:T(1024)(128)(2,1)S(1)} %bitcast.159, s32[1024]{0:T(1024)S(1)} %pad_clamp_fusion.3), kind=kCustom, calls=%fused_computation.1.clone | custom fusion | bytes 4096 | tf_op jit(solution)/shard_map/jit(_take)/gather | solution.py:79
  113.2 3.5 %gather_fusion.4 = bf16[512]{0:T(512)(128)(2,1)S(1)} fusion(bf16[131072]{0:T(1024)(128)(2,1)S(1)} %bitcast.150, s32[1024]{0:T(1024)S(1)} %pad_clamp_fusion.3), kind=kCustom, calls=%fused_computation.clone | custom fusion | bytes 4096 | tf_op jit(solution)/shard_map/jit(_take)/gather | solution.py:79
  116.7 2.3 gather_fusion
  119.0 3.3 %gather_fusion.1 = f32[512]{0:T(512)S(1)} fusion(f32[128]{0:T(128)S(1)} %multiply_add_fusion.1, s32[1024]{0:T(1024)S(1)} %pad_clamp_fusion.1), kind=kCustom, calls=%fused_computation.13 | custom fusion | bytes 6144 | tf_op jit(solution)/shard_map/gather | solution.py:83
  122.4 1.1 fusion.45
  123.6 3.1 %gather_fusion.3 = f32[512]{0:T(512)S(1)} fusion(f32[131072]{0:T(1024)S(1)} %bitcast.147, s32[1024]{0:T(1024)S(1)} %pad_clamp_fusion), kind=kCustom, calls=%fused_computation.15 | custom fusion | bytes 6144 | tf_op jit(solution)/shard_map/jit(_take)/gather | solution.py:59
  128.1 1.4 cholesky.16
  130.8 1.2 custom-call.10
  134.3 10.7 %fusion.181 = (f32[128,1024]{1,0:T(8,128)}, f32[128,1024]{1,0:T(8,128)S(1)}) fusion(f32[1024]{0:T(1024)S(1)} %bitcast.174, f32[128,1024]{1,0:T(8,128)S(1)} %copy-done, f32[]{:T(128)} %bitcast.27, f32[128]{0:T(128)S(1)} %broadcast_multiply_fusion.1, f32[1024]{0:T(1024)S(1)} %broadcast_multiply_fusion, f32[]{:T(128)} %bitcast.48, ...), kind=kLoop, calls=%fused_computation.250 | loop fusion | flops 5636096 | bytes 4727356 | tf_op jit(solution)/shard_map/mul | solution.py:96
  145.0 88.2 %all-reduce.7.cloned.1.call-done = f32[128,1024]{1,0:T(8,128)} async-done(((f32[128,1024]{1,0:T(8,128)}), f32[128,1024]{1,0:T(8,128)}) %all-reduce.7.cloned.1.call-update) | async-done | bytes 524304 | tf_op jit(solution)/shard_map/psum | solution.py:96
  233.2 1.9 multiply_bitcast_fusion
  (73 shorter events, 8.8 us)
Async XLA Ops:
  7.2 115.3 %all-reduce.5.cloned.1.call-start = ((), (), s32[]{:S(2)}) async-start(), calls=%async_computation | async-start | bytes 1048576 | tf_op jit(solution)/shard_map/psum | solution.py:56
  10.8 222.4 %all-reduce.7.cloned.1.call-start = ((), (), s32[]{:S(2)}) async-start(), calls=%async_computation.1 | async-start | bytes 1048576 | tf_op jit(solution)/shard_map/psum | solution.py:96
  25.2 70.0 %copy-start.1 = (bf16[128,1024]{1,0:T(8,128)(2,1)}, bf16[128,1024]{1,0:T(8,128)(2,1)S(1)}, u32[]{:S(2)}) copy-start(bf16[128,1024]{1,0:T(8,128)(2,1)S(1)} %fusion.21) | copy-start | bytes 786436
  34.0 1.1 copy-start.7
  34.0 38.8 %copy-start.6 = (s32[4]{0:T(128)S(1)}, s32[4]{0:T(128)}, u32[]{:S(2)}) copy-start(s32[4]{0:T(128)} %param.13) | copy-start | bytes 52
  34.0 39.0 %copy-start.5 = (s32[1,512]{1,0:T(1,128)S(1)}, s32[1,512]{1,0:T(1,128)}, u32[]{:S(2)}) copy-start(s32[1,512]{1,0:T(1,128)} %param.12) | copy-start | bytes 6148
  98.9 3.5 %copy-start.2 = (bf16[128,1024]{1,0:T(8,128)(2,1)S(1)}, bf16[128,1024]{1,0:T(8,128)(2,1)}, u32[]{:S(2)}) copy-start(bf16[128,1024]{1,0:T(8,128)(2,1)} %fusion.25) | copy-start | bytes 786436
  106.0 3.5 %copy-start.3 = (bf16[128,1024]{1,0:T(8,128)(2,1)S(1)}, bf16[128,1024]{1,0:T(8,128)(2,1)}, u32[]{:S(2)}) copy-start(bf16[128,1024]{1,0:T(8,128)(2,1)} %fusion.28) | copy-start | bytes 786436
  126.8 7.5 %copy-start = (f32[128,1024]{1,0:T(8,128)S(1)}, f32[128,1024]{1,0:T(8,128)}, u32[]{:S(2)}) copy-start(f32[128,1024]{1,0:T(8,128)} %all-reduce.5.cloned.1.call-done) | copy-start | bytes 1572868
  132.3 12.7 %copy-start.4 = (f32[1,15]{1,0:T(1,128)}, f32[1,15]{1,0:T(1,128)S(1)}, u32[]{:S(2)}) copy-start(f32[1,15]{1,0:T(1,128)S(1)} %fusion.71) | copy-start | bytes 184
Sparse Core Ops, SparseCore 0:
  11.9 93.5 all-reduce.4
  145.1 88.0 all-reduce.6
where the time goes:
time: 242 us
  waiting for transfers between devices  88.2 us (36%)
  local copies, waits for them, and re-layouts  54.6 us (23%)
  blocking collectives  36.3 us (15%)
  matrix products  24.1 us (10%)
  other arithmetic  21.4 us (9%)
  between operations  17.2 us (7%)
    psum x1, waiting for transfers between devices, shards(): pooled = lax.psum(diff * diff, 'epoch')  88.2 us
    gather x12, local copies, waits for them, and re-layouts, shards(): jnp.take(b.reshape(-1), stamp_row).astype(jnp.float32)  42.2 us
    unnamed x1, blocking collectives  36.3 us
    dot_general x12, matrix products, shards(): jnp.dot(vertical, across[pair[0]], preferred_element_type=jnp.float32)  17 us
    mul x1, other arithmetic, shards(): pooled = lax.psum(diff * diff, 'epoch')  10.7 us
    dot_general x3, matrix products, shards(): jnp.dot(sharp, band_matrix(cols_all, sigma, degree, True), preferred_elem...  6.5 us
  transfers between devices with their start and end apart: 2, of which 1 were waited for; matrix products, arithmetic and copies ran while one was open for 30% of the time, Pallas kernels for 0%

commit v1 on v0

--- a/solution.py
+++ b/solution.py
@@ -93,7 +93,7 @@
         model = model + coef[index] * bases[index].astype(jnp.float32)
     model = model + coef[NBASIS] + coef[NBASIS + 1] * xn[None, :] + coef[NBASIS + 2] * yn[:, None]
     diff = jnp.repeat(mask_f, 128)[:, None] * (model - reference_img)
-    pooled = lax.psum(diff * diff, "epoch")
+    pooled = jnp.sum(lax.all_gather(diff * diff, "epoch"), axis=0)
     scatter = jnp.sqrt(0.05 + pooled / count)
     result = diff / scatter
     return (result[None], coef[None])

time: 242 us -> 229 us (0.946)
  waiting for transfers between devices: 88.2 us -> 71.8 us
  other arithmetic: 21.4 us -> 24.6 us
    psum x1 -> x0, waiting for transfers between devices: 88.2 us -> none  [shards(): pooled = lax.psum(diff * diff, 'epoch')]
    all_gather x0 -> x1, waiting for transfers between devices: none -> 71.7 us  [shards(): pooled = jnp.sum(lax.all_gather(diff * diff, 'epoch'), axis=0)]
    reduce_sum x0 -> x1, other arithmetic: none -> 4.24 us  [shards(): pooled = jnp.sum(lax.all_gather(diff * diff, 'epoch'), axis=0)]
  transfers between devices with their start and end apart: 2 -> 2, of which waited for: 1 -> 1; matrix products, arithmetic and copies ran while one was open for 30% -> 32% of each run, Pallas kernels for 0% -> 0%
where the time goes in v1:
time: 229 us
  waiting for transfers between devices  71.8 us (31%)
  local copies, waits for them, and re-layouts  55.6 us (24%)
  blocking collectives  36.3 us (16%)
  other arithmetic  24.6 us (11%)
  matrix products  23.4 us (10%)
  between operations  17.2 us (8%)
    all_gather x1, waiting for transfers between devices, shards(): pooled = jnp.sum(lax.all_gather(diff * diff, 'epoch'), axis=0)  71.7 us
    gather x12, local copies, waits for them, and re-layouts, shards(): jnp.take(b.reshape(-1), stamp_row).astype(jnp.float32)  42.2 us
    unnamed x1, blocking collectives  36.3 us
    dot_general x12, matrix products, shards(): jnp.dot(vertical, across[pair[0]], preferred_element_type=jnp.float32)  16.1 us
    mul x1, other arithmetic, shards(): pooled = jnp.sum(lax.all_gather(diff * diff, 'epoch'), axis=0)  10.7 us
    dot_general x3, matrix products, shards(): jnp.dot(sharp, band_matrix(cols_all, sigma, degree, True), preferred_elem...  6.67 us
  transfers between devices with their start and end apart: 2, of which 1 were waited for; matrix products, arithmetic and copies ran while one was open for 32% of the time, Pallas kernels for 0%

profile of v1, /device:TPU:0, one launch (start us, length us, event | category | flops | bytes accessed | tf_op | source)
XLA Modules:
  0.0 228.9 jit_solution(13769973543355352366)
XLA Ops:
  8.5 2.1 fusion.182
  10.7 2.4 %fusion.28 = bf16[128,1024]{1,0:T(8,128)(2,1)S(1)} fusion(bf16[1,128,1024]{2,1,0:T(8,128)(2,1)S(1)} %get-tuple-element.11), kind=kOutput, calls=%fused_computation.61 | convolution fusion | flops 314998784 | bytes 524288 | tf_op jit(solution)/shard_map/dot_general | solution.py:73
  13.1 2.3 fusion.25
  15.4 2.2 fusion.22
  18.1 2.4 %fusion.21 = bf16[128,1024]{1,0:T(8,128)(2,1)S(1)} fusion(bf16[1,128,1024]{2,1,0:T(8,128)(2,1)S(1)} %get-tuple-element.11), kind=kOutput, calls=%fused_computation.54 | convolution fusion | flops 314998784 | bytes 524288 | tf_op jit(solution)/shard_map/dot_general | solution.py:73
  20.5 2.3 fusion.18
  22.8 2.3 %fusion.15 = bf16[1024,128]{1,0:T(8,128)(2,1)S(1)} fusion(bf16[1,128,1024]{2,1,0:T(8,128)(2,1)S(1)} %get-tuple-element.11), kind=kOutput, calls=%fused_computation.48 | convolution fusion | flops 279052288 | bytes 524288 | tf_op jit(solution)/shard_map/dot_general | solution.py:65
  25.6 2.4 %fusion.14 = bf16[128,1024]{1,0:T(8,128)(2,1)S(1)} fusion(bf16[1,128,1024]{2,1,0:T(8,128)(2,1)S(1)} %get-tuple-element.11), kind=kOutput, calls=%fused_computation.47 | convolution fusion | flops 314998784 | bytes 524288 | tf_op jit(solution)/shard_map/dot_general | solution.py:73
  28.0 3.0 %fusion.11 = bf16[128,1024]{1,0:T(8,128)(2,1)} fusion(bf16[1,128,1024]{2,1,0:T(8,128)(2,1)S(1)} %get-tuple-element.11), kind=kOutput, calls=%fused_computation.44 | convolution fusion | flops 313966592 | bytes 524288 | tf_op jit(solution)/shard_map/dot_general | solution.py:73
  31.0 2.2 fusion.29
  35.7 36.3 %all-reduce.1 = (f32[16]{0:T(128)S(1)}, f32[1]{0:T(128)}) all-reduce(f32[16]{0:T(128)S(1)} %dynamic-update-slice.3, f32[1]{0:T(128)} %mul.385), channel_id=1, replica_groups=mesh['patch'=2,'epoch'=16] {'epoch'}, use_global_device_ids=true, to_apply=%add | all-reduce | flops 17 | bytes 136
  73.1 3.5 %gather_fusion.6 = bf16[512]{0:T(512)(128)(2,1)S(1)} fusion(bf16[131072]{0:T(1024)(128)(2,1)S(1)} %bitcast.151, s32[1024]{0:T(1024)S(1)} %pad_clamp_fusion.3), kind=kCustom, calls=%fused_computation.2.clone | custom fusion | bytes 4096 | tf_op jit(solution)/shard_map/jit(_take)/gather | solution.py:79
  76.7 3.5 %gather_fusion.4 = bf16[512]{0:T(512)(128)(2,1)S(1)} fusion(bf16[131072]{0:T(1024)(128)(2,1)S(1)} %bitcast.150, s32[1024]{0:T(1024)S(1)} %pad_clamp_fusion.3), kind=kCustom, calls=%fused_computation.clone | custom fusion | bytes 4096 | tf_op jit(solution)/shard_map/jit(_take)/gather | solution.py:79
  81.2 3.5 %gather_fusion.15 = bf16[512]{0:T(512)(128)(2,1)S(1)} fusion(bf16[131072]{0:T(1024)(128)(2,1)S(1)} %bitcast.153, s32[1024]{0:T(1024)S(1)} %pad_clamp_fusion.3), kind=kCustom, calls=%fused_computation.11.clone | custom fusion | bytes 4096 | tf_op jit(solution)/shard_map/jit(_take)/gather | solution.py:79
  84.8 3.5 %gather_fusion.13 = bf16[512]{0:T(512)(128)(2,1)S(1)} fusion(bf16[131072]{0:T(1024)(128)(2,1)S(1)} %bitcast.154, s32[1024]{0:T(1024)S(1)} %pad_clamp_fusion.3), kind=kCustom, calls=%fused_computation.9.clone | custom fusion | bytes 4096 | tf_op jit(solution)/shard_map/jit(_take)/gather | solution.py:79
  88.3 3.5 %gather_fusion.14 = bf16[512]{0:T(512)(128)(2,1)S(1)} fusion(bf16[131072]{0:T(1024)(128)(2,1)S(1)} %bitcast.155, s32[1024]{0:T(1024)S(1)} %pad_clamp_fusion.3), kind=kCustom, calls=%fused_computation.10.clone | custom fusion | bytes 4096 | tf_op jit(solution)/shard_map/jit(_take)/gather | solution.py:79
  91.9 3.5 %gather_fusion.12 = bf16[512]{0:T(512)(128)(2,1)S(1)} fusion(bf16[131072]{0:T(1024)(128)(2,1)S(1)} %bitcast.156, s32[1024]{0:T(1024)S(1)} %pad_clamp_fusion.3), kind=kCustom, calls=%fused_computation.8.clone | custom fusion | bytes 4096 | tf_op jit(solution)/shard_map/jit(_take)/gather | solution.py:79
  95.5 3.5 %gather_fusion.11 = bf16[512]{0:T(512)(128)(2,1)S(1)} fusion(bf16[131072]{0:T(1024)(128)(2,1)S(1)} %bitcast.157, s32[1024]{0:T(1024)S(1)} %pad_clamp_fusion.3), kind=kCustom, calls=%fused_computation.7.clone | custom fusion | bytes 4096 | tf_op jit(solution)/shard_map/jit(_take)/gather | solution.py:79
  99.1 3.5 %gather_fusion.9 = bf16[512]{0:T(512)(128)(2,1)S(1)} fusion(bf16[131072]{0:T(1024)(128)(2,1)S(1)} %bitcast.158, s32[1024]{0:T(1024)S(1)} %pad_clamp_fusion.3), kind=kCustom, calls=%fused_computation.5.clone | custom fusion | bytes 4096 | tf_op jit(solution)/shard_map/jit(_take)/gather | solution.py:79
  102.6 3.5 %gather_fusion.10 = bf16[512]{0:T(512)(128)(2,1)S(1)} fusion(bf16[131072]{0:T(1024)(128)(2,1)S(1)} %bitcast.159, s32[1024]{0:T(1024)S(1)} %pad_clamp_fusion.3), kind=kCustom, calls=%fused_computation.6.clone | custom fusion | bytes 4096 | tf_op jit(solution)/shard_map/jit(_take)/gather | solution.py:79
  106.2 3.5 %gather_fusion.8 = bf16[512]{0:T(512)(128)(2,1)S(1)} fusion(bf16[131072]{0:T(1024)(128)(2,1)S(1)} %bitcast.160, s32[1024]{0:T(1024)S(1)} %pad_clamp_fusion.3), kind=kCustom, calls=%fused_computation.4.clone | custom fusion | bytes 4096 | tf_op jit(solution)/shard_map/jit(_take)/gather | solution.py:79
  109.8 3.5 %gather_fusion.7 = bf16[512]{0:T(512)(128)(2,1)S(1)} fusion(bf16[131072]{0:T(1024)(128)(2,1)S(1)} %bitcast.161, s32[1024]{0:T(1024)S(1)} %pad_clamp_fusion.3), kind=kCustom, calls=%fused_computation.3.clone | custom fusion | bytes 4096 | tf_op jit(solution)/shard_map/jit(_take)/gather | solution.py:79
  113.4 3.5 %gather_fusion.5 = bf16[512]{0:T(512)(128)(2,1)S(1)} fusion(bf16[131072]{0:T(1024)(128)(2,1)S(1)} %bitcast.152, s32[1024]{0:T(1024)S(1)} %pad_clamp_fusion.3), kind=kCustom, calls=%fused_computation.1.clone | custom fusion | bytes 4096 | tf_op jit(solution)/shard_map/jit(_take)/gather | solution.py:79
  116.9 3.3 %gather_fusion.1 = f32[512]{0:T(512)S(1)} fusion(f32[128]{0:T(128)S(1)} %multiply_add_fusion.1, s32[1024]{0:T(1024)S(1)} %pad_clamp_fusion.1), kind=kCustom, calls=%fused_computation.13 | custom fusion | bytes 6144 | tf_op jit(solution)/shard_map/gather | solution.py:83
  120.2 2.3 gather_fusion
  122.6 1.2 fusion.45
  123.9 3.1 %gather_fusion.3 = f32[512]{0:T(512)S(1)} fusion(f32[131072]{0:T(1024)S(1)} %bitcast.148, s32[1024]{0:T(1024)S(1)} %pad_clamp_fusion), kind=kCustom, calls=%fused_computation.15 | custom fusion | bytes 6144 | tf_op jit(solution)/shard_map/jit(_take)/gather | solution.py:59
  128.4 1.4 cholesky.16
  131.1 1.2 custom-call.10
  134.5 10.7 %fusion.181 = (f32[128,1024]{1,0:T(8,128)}, f32[128,1024]{1,0:T(8,128)S(1)}) fusion(f32[1024]{0:T(1024)S(1)} %bitcast.176, f32[128,1024]{1,0:T(8,128)S(1)} %copy-done, f32[]{:T(128)} %bitcast.27, f32[128]{0:T(128)S(1)} %broadcast_multiply_fusion.1, f32[1024]{0:T(1024)S(1)} %broadcast_multiply_fusion, f32[]{:T(128)} %bitcast.48, ...), kind=kLoop, calls=%fused_computation.250 | loop fusion | flops 5636096 | bytes 4727356 | tf_op jit(solution)/shard_map/mul | solution.py:96
  145.3 71.7 %all-gather.3.cloned.1.call-done = f32[2048,1024]{1,0:T(8,128)} async-done(((f32[128,1024]{1,0:T(8,128)}), f32[2048,1024]{1,0:T(8,128)}) %all-gather.3.cloned.1.call-update) | async-done | bytes 8388624 | tf_op jit(solution)/shard_map/all_gather | solution.py:96
  217.0 4.2 %reduce_sum.19 = f32[128,1024]{1,0:T(8,128)S(1)} reduce(f32[16,128,1024]{2,1,0:T(8,128)} %bitcast.149, f32[]{:T(128)} %constant.175.clone.1), dimensions={0}, to_apply=%region_5.7 | reduce | flops 1966080 | bytes 8912900 | tf_op jit(solution)/shard_map/reduce_sum | solution.py:96
  (72 shorter events, 10.6 us)
Async XLA Ops:
  7.2 115.4 %all-reduce.4.cloned.1.call-start = ((), (), s32[]{:S(2)}) async-start(), calls=%async_computation | async-start | bytes 1048576 | tf_op jit(solution)/shard_map/psum | solution.py:56
  10.7 206.3 %all-gather.3.cloned.1.call-start = ((), (), s32[]{:S(2)}) async-start(), calls=%async_computation.1 | async-start | bytes 8912896 | tf_op jit(solution)/shard_map/all_gather | solution.py:96
  22.8 72.7 %copy-start.1 = (bf16[128,1024]{1,0:T(8,128)(2,1)}, bf16[128,1024]{1,0:T(8,128)(2,1)S(1)}, u32[]{:S(2)}) copy-start(bf16[128,1024]{1,0:T(8,128)(2,1)S(1)} %fusion.18) | copy-start | bytes 786436
  28.0 56.7 %copy-start.2 = (bf16[128,1024]{1,0:T(8,128)(2,1)}, bf16[128,1024]{1,0:T(8,128)(2,1)S(1)}, u32[]{:S(2)}) copy-start(bf16[128,1024]{1,0:T(8,128)(2,1)S(1)} %fusion.14) | copy-start | bytes 786436
  31.0 3.3 %copy-start.6 = (u32[32]{0:T(128)S(1)}, u32[32]{0:T(128)}, u32[]{:S(2)}) copy-start(u32[32]{0:T(128)} %constant.221) | copy-start | bytes 388
  31.0 41.0 %copy-start.4 = (s32[1,512]{1,0:T(1,128)S(1)}, s32[1,512]{1,0:T(1,128)}, u32[]{:S(2)}) copy-start(s32[1,512]{1,0:T(1,128)} %param.12) | copy-start | bytes 6148
  31.0 41.1 %copy-start.5 = (s32[4]{0:T(128)S(1)}, s32[4]{0:T(128)}, u32[]{:S(2)}) copy-start(s32[4]{0:T(128)} %param.13) | copy-start | bytes 52
  122.6 11.9 %copy-start = (f32[128,1024]{1,0:T(8,128)S(1)}, f32[128,1024]{1,0:T(8,128)}, u32[]{:S(2)}) copy-start(f32[128,1024]{1,0:T(8,128)} %all-reduce.4.cloned.1.call-done) | copy-start | bytes 1572868
  132.5 88.7 %copy-start.3 = (f32[1,15]{1,0:T(1,128)}, f32[1,15]{1,0:T(1,128)S(1)}, u32[]{:S(2)}) copy-start(f32[1,15]{1,0:T(1,128)S(1)} %fusion.71) | copy-start | bytes 184
Sparse Core Ops, SparseCore 0:
  11.9 93.5 all-reduce.3
  145.4 71.5 all-gather.2
